TPU v7x, 32 devices: a whole 2x2x4 slice. The times are simulated.
32 devices in a mesh: group: 2 (over y), tm: 4 (over z), seq: 2 (over x), mp: 2 (over core).
Axes of the slice: x: 2, y: 2, z: 4, core: 2. Of those that a mesh axis runs over, the one named last changes fastest.
Arguments:
- states: bfloat16 [8, 128, 5120], P(('group', 'tm'), 'seq'), parts along dimension 0, may hold values from -6 to 6
- start_step: int32 [2], P('group'), parts along dimension 0, may hold values from 0 to 96
- w_qkv: bfloat16 [3, 5120, 3072], P(None, 'tm', ('seq', 'mp')), may hold values from -0.078125 to 0.078125
- qk_gain: float32 [2, 3072], P(None, ('seq', 'mp')), may hold values from 0.25 to 1.75
- w_out: bfloat16 [5120, 3072], P('tm', ('seq', 'mp')), may hold values from -0.109375 to 0.109375
- time_proj: bfloat16 [256, 15360], P('tm'), may hold values from -0.375 to 0.375
Outputs:
- displacement: float32 [8, 128, 5120], P(('group', 'tm'), 'seq', 'mp'), parts along dimension 0
There are 2 independent parts, one for each index of `group`. A program takes and returns all parts, laid end to end along the dimension named above; an argument that names none is the same for every part. Nothing has to cross between parts.
Inputs may be any that keep to these rules, and one draw needn't show every extreme that they name: `start_step`: the window lies inside the trajectory.
All inputs are finite; a program needn't handle non-finite values.
Results may differ from a plain program's by a relative error of at most 0.0029.
Values may be sent and summed in bfloat16 or wider, within the bound.
No kernel may reach another device: no remote copies, remote signals or barrier semaphores. Data moves between devices by JAX's collectives and lax.ppermute only.
A program may use at most 128 MiB of HBM per device.

v0:
```python
import jax
import jax.numpy as jnp
from jax import lax
from jax.sharding import PartitionSpec as P

HEAD_DIM = 128
FREQ = 256
STEPS = 100
sample_shift = 5.0
norm_eps = 1e-06


def from_behind(block, axis, distance):
    devices = range(lax.axis_size(axis))
    route = [(i - distance, i) for i in devices if i - distance in devices]
    return lax.ppermute(block, axis, route)


def sigma_of(index):
    unit = 1.0 - index.astype(jnp.float32) / jnp.float32(STEPS)
    return sample_shift * unit / (1.0 + (sample_shift - 1.0) * unit)


def embed_time(sigma_now):
    half_freq = FREQ // 2
    ranks = jnp.arange(half_freq).astype(jnp.float32)
    freqs = jnp.exp(-jnp.log(jnp.float32(10000.0)) * ranks / jnp.float32(half_freq))
    angles = (1000.0 * sigma_now)[:, None] * freqs[None, :]
    return jnp.concatenate([jnp.cos(angles), jnp.sin(angles)], axis=1).astype(jnp.bfloat16)


def head_norm(values, gain, frames, seq_len, heads_dev):
    shaped = values.reshape(frames, seq_len, heads_dev, HEAD_DIM)
    meansq = jnp.mean(shaped * shaped, axis=-1, keepdims=True)
    scaled = shaped * lax.rsqrt(meansq + norm_eps) * gain.reshape(heads_dev, HEAD_DIM)
    return scaled.astype(jnp.bfloat16)


def attend(query, keys, values):
    frames, seq_len, heads_dev, head_size = query.shape
    block = min(seq_len, 512)
    blocks = seq_len // block
    inv_root = 1.0 / jnp.sqrt(jnp.float32(head_size))
    stacked = query.reshape(frames, blocks, block, heads_dev, head_size).transpose(1, 0, 2, 3, 4)

    def one_block(q_block):
        scores = (
            jnp.einsum("wqhd,wkhd->whqk", q_block, keys, preferred_element_type=jnp.float32)
            * inv_root
        )
        expo = jnp.exp(scores)
        probs = (expo / jnp.sum(expo, axis=-1, keepdims=True)).astype(jnp.bfloat16)
        return jnp.einsum(
            "whqk,wkhd->wqhd", probs, values, preferred_element_type=jnp.float32
        ).astype(jnp.bfloat16)

    result = lax.map(one_block, stacked)
    return result.transpose(1, 0, 2, 3, 4).reshape(frames, seq_len, heads_dev * head_size)


def on_device(states, start_step, w_qkv, qk_gain, w_out, time_proj):
    frames, tok, width = states.shape
    n_tm = lax.axis_size("tm")
    n_mp = lax.axis_size("mp")
    window = frames * n_tm
    tm_pos = lax.axis_index("tm")
    steps_idx = start_step[0] + jnp.arange(window)
    sigma_now = sigma_of(steps_idx)
    step_size = sigma_of(steps_idx + 1) - sigma_now
    emb = embed_time(sigma_now)
    freq_rows = time_proj.shape[0]
    emb_cols = lax.dynamic_slice_in_dim(emb, tm_pos * freq_rows, freq_rows, 1)
    modulation = lax.psum_scatter(
        jnp.dot(emb_cols, time_proj, preferred_element_type=jnp.float32),
        "tm",
        scatter_dimension=0,
        tiled=True,
    )
    shift = modulation[:, :width]
    scale = modulation[:, width : 2 * width]
    gate = modulation[:, 2 * width :]
    field = states.astype(jnp.float32)
    mean = jnp.mean(field, axis=-1, keepdims=True)
    centred = field - mean
    var = jnp.mean(centred * centred, axis=-1, keepdims=True)
    normed = centred * lax.rsqrt(var + norm_eps)
    hidden = (normed * (1.0 + scale[:, None, :]) + shift[:, None, :]).astype(jnp.bfloat16)
    whole = lax.all_gather(hidden, "seq", axis=1, tiled=True)
    seq_len = whole.shape[1]
    flat = whole.reshape(frames * seq_len, width)
    head_cols = w_qkv.shape[2]
    heads_dev = head_cols // HEAD_DIM
    proj = jnp.einsum(
        "rd,cdh->crh",
        flat,
        lax.all_gather(w_qkv, "tm", axis=1, tiled=True),
        preferred_element_type=jnp.float32,
    )
    query = head_norm(proj[0], qk_gain[0], frames, seq_len, heads_dev)
    keys = head_norm(proj[1], qk_gain[1], frames, seq_len, heads_dev)
    values = proj[2].astype(jnp.bfloat16).reshape(frames, seq_len, heads_dev, HEAD_DIM)
    attn = attend(query, keys, values)
    out_full = lax.all_gather(w_out, "tm", axis=0, tiled=True)
    half_width = width // n_mp
    rows = frames * tok
    first = jnp.int32(0) // rows
    pieces = []
    for offset in range(rows * lax.axis_size(("seq", "mp")) // rows):
        owner = first + offset
        segment = owner // n_mp
        column = owner % n_mp
        tokens_part = lax.dynamic_slice_in_dim(attn, segment * tok, tok, 1)
        weight_part = lax.dynamic_slice_in_dim(out_full, column * half_width, half_width, 0)
        product = jnp.einsum(
            "tsh,eh->tse", tokens_part, weight_part, preferred_element_type=jnp.float32
        )
        pieces.append(product.reshape(rows, half_width))
    out_part = lax.psum_scatter(
        jnp.concatenate(pieces, axis=0), ("seq", "mp"), scatter_dimension=0, tiled=True
    ).reshape(frames, tok, half_width)
    gate_own = lax.dynamic_slice_in_dim(gate, lax.axis_index("mp") * half_width, half_width, 1)
    own_steps = lax.dynamic_slice_in_dim(step_size, tm_pos * frames, frames, 0)
    drift = gate_own[:, None, :] * out_part
    increments = own_steps[:, None, None] * drift
    local_sums = jnp.cumsum(increments, axis=0)
    block_total = local_sums[-1]
    running = block_total
    for level in range((n_tm - 1).bit_length()):
        running = running + from_behind(running, "tm", 1 << level)
    before = running - block_total
    return before[None, :, :] + local_sums


def solution(mesh):
    return jax.shard_map(
        on_device,
        mesh=mesh,
        in_specs=(
            P(("group", "tm"), "seq", None),
            P("group"),
            P(None, "tm", ("seq", "mp")),
            P(None, ("seq", "mp")),
            P("tm", ("seq", "mp")),
            P("tm", None),
        ),
        out_specs=P(("group", "tm"), "seq", "mp"),
        check_vma=False,
    )
```

profile of v0, /device:TPU:25, one launch (start us, length us, event | category | flops | bytes accessed | tf_op | source)
XLA Modules:
  0.0 721.7 jit_solution(13477119722304982495)
XLA Ops:
  8.3 1.1 fusion.26
  10.7 32.4 %all-reduce.3.cloned.1.call-done = f32[4,15360]{1,0:T(4,128)} async-done(((f32[4,15360]{1,0:T(4,128)}), f32[4,15360]{1,0:T(4,128)}) %all-reduce.3.cloned.1.call-update) | async-done | bytes 245776
  43.0 1.7 dynamic-slice_add_fusion
  44.7 1.1 fusion.13
  47.3 25.9 %all-gather.4.cloned.1.call-done = bf16[1,128,5120]{2,1,0:T(8,128)(2,1)} async-done(((bf16[1,64,5120]{2,1,0:T(8,128)(2,1)}), bf16[1,128,5120]{2,1,0:T(8,128)(2,1)}) %all-gather.4.cloned.1.call-update) | async-done | bytes 1310736 | tf_op jit(solution)/shard_map/all_gather | solution.py:88
  73.2 398.3 %all-gather.6.cloned.1.call-done = bf16[3,5120,768]{2,1,0:T(8,128)(2,1)} async-done(((bf16[3,1280,768]{2,1,0:T(8,128)(2,1)}), bf16[3,5120,768]{2,1,0:T(8,128)(2,1)}) %all-gather.6.cloned.1.call-update) | async-done | bytes 23592976 | tf_op jit(solution)/shard_map/all_gather | solution.py:96
  471.4 10.0 %convolution_bitcast_fusion = f32[3,128,768]{2,1,0:T(8,128)S(1)} fusion(bf16[3,5120,768]{2,1,0:T(8,128)(2,1)} %all-gather.6.cloned.1.call-done, bf16[1,128,5120]{2,1,0:T(8,128)(2,1)} %all-gather.4.cloned.1.call-done), kind=kOutput, calls=%fused_computation.13 | convolution fusion | flops 3019898880 | bytes 26083328 | tf_op jit(solution)/shard_map/rd,cdh->crh/dot_general | solution.py:93
  483.3 1.1 reduce_sum.49
  484.8 1.1 copy.19
  486.7 125.4 %all-gather.8.cloned.1.call-done = bf16[5120,768]{1,0:T(8,128)(2,1)} async-done(((bf16[1280,768]{1,0:T(8,128)(2,1)}), bf16[5120,768]{1,0:T(8,128)(2,1)}) %all-gather.8.cloned.1.call-update) | async-done | bytes 7864336 | tf_op jit(solution)/shard_map/all_gather | solution.py:103
  612.1 3.6 fusion.2
  615.7 3.6 fusion.4
  619.3 1.3 fusion.6
  620.6 1.5 fusion
  622.1 1.7 pad_maximum_fusion
  624.9 1.5 dynamic-slice_reduce_fusion
  626.4 32.9 %reduce-scatter.2.cloned.1.call-done = f32[64,2560]{1,0:T(8,128)} async-done(((f32[256,2560]{1,0:T(8,128)}), f32[64,2560]{1,0:T(8,128)}) %reduce-scatter.2.cloned.1.call-update) | async-done | bytes 655376 | tf_op jit(solution)/shard_map/reduce_scatter | solution.py:118
  659.4 1.8 multiply_multiply_fusion
  661.1 1.3 collective-permute-start
  662.4 16.1 %collective-permute-done = f32[64,2560]{1,0:T(8,128)S(1)} collective-permute-done((f32[64,2560]{1,0:T(8,128)S(1)}, f32[64,2560]{1,0:T(8,128)S(1)}, u32[]{:S(2)}, u32[]{:S(2)}) %collective-permute-start) | collective-permute-done | bytes 655392 | tf_op jit(solution)/shard_map/ppermute | solution.py:16
  678.5 1.7 fusion.35
  680.2 1.3 collective-permute-start.1
  681.5 32.1 %collective-permute-done.1 = f32[64,2560]{1,0:T(8,128)S(1)} collective-permute-done((f32[64,2560]{1,0:T(8,128)S(1)}, f32[64,2560]{1,0:T(8,128)S(1)}, u32[]{:S(2)}, u32[]{:S(2)}) %collective-permute-start.1) | collective-permute-done | bytes 655392 | tf_op jit(solution)/shard_map/ppermute | solution.py:16
  713.7 1.5 fusion.16
  (45 shorter events, 7.7 us)
Async XLA Ops:
  6.5 1.8 copy-start
  6.5 3.5 copy-start.6
  6.5 3.0 copy-start.2
  6.5 36.5 %all-reduce.3.cloned.1.call-start = ((), (), s32[]{:S(2)}) async-start(), calls=%async_computation.5 | async-start | bytes 491520
  9.5 63.7 %all-gather.4.cloned.1.call-start = ((), (), s32[]{:S(2)}) async-start(), calls=%async_computation.1 | async-start | bytes 1966080 | tf_op jit(solution)/shard_map/all_gather | solution.py:88
  45.9 1.4 copy-start.4
  45.9 425.6 %all-gather.6.cloned.1.call-start = ((), (), s32[]{:S(2)}) async-start(), calls=%async_computation.2 | async-start | bytes 29491200 | tf_op jit(solution)/shard_map/all_gather | solution.py:96
  46.6 565.5 %all-gather.8.cloned.1.call-start = ((), (), s32[]{:S(2)}) async-start(), calls=%async_computation.3 | async-start | bytes 9830400 | tf_op jit(solution)/shard_map/all_gather | solution.py:103
  47.2 612.2 %reduce-scatter.2.cloned.1.call-start = ((), (), s32[]{:S(2)}) async-start(), calls=%async_computation.4 | async-start | bytes 3276800 | tf_op jit(solution)/shard_map/reduce_scatter | solution.py:118
  612.1 7.1 copy-start.1
  623.8 0.6 copy-start.5
  659.4 54.3 %copy-start.3 = (f32[64,2560]{1,0:T(8,128)S(1)}, f32[64,2560]{1,0:T(8,128)}, u32[]{:S(2)}) copy-start(f32[64,2560]{1,0:T(8,128)} %reduce-scatter.2.cloned.1.call-done) | copy-start | bytes 1966084
  661.1 17.4 %collective-permute-start = (f32[64,2560]{1,0:T(8,128)S(1)}, f32[64,2560]{1,0:T(8,128)S(1)}, u32[]{:S(2)}, u32[]{:S(2)}) collective-permute-start(f32[64,2560]{1,0:T(8,128)S(1)} %multiply_multiply_fusion), channel_id=1, source_target_pairs={{0,4},{4,8},{8,12},{1,5},{5,9},{9,13},{2,6},{6,10},{10,14},{3,7},{... | collective-permute-start | bytes 1966088 | tf_op jit(solution)/shard_map/ppermute | solution.py:16
  680.2 33.4 %collective-permute-start.1 = (f32[64,2560]{1,0:T(8,128)S(1)}, f32[64,2560]{1,0:T(8,128)S(1)}, u32[]{:S(2)}, u32[]{:S(2)}) collective-permute-start(f32[64,2560]{1,0:T(8,128)S(1)} %fusion.35), channel_id=1, source_target_pairs={{0,8},{4,12},{1,9},{5,13},{2,10},{6,14},{3,11},{7,15},{16,24},{20,... | collective-permute-start | bytes 1966088 | tf_op jit(solution)/shard_map/ppermute | solution.py:16
Sparse Core Ops, SparseCore 0:
  9.7 33.3 all-reduce.2
  46.0 27.1 all-gather.3
  74.7 396.6 all-gather.5
  472.9 139.2 all-gather.7
  623.9 35.4 reduce-scatter.1
where the time goes:
time: 722 us
  waiting for transfers between devices  664 us (92%)
  matrix products  21.8 us (3%)
  between operations  14.1 us (2%)
  other arithmetic  12 us (2%)
    all_gather x1, waiting for transfers between devices, on_device(): lax.all_gather(w_qkv, 'tm', axis=1, tiled=True)  398 us
    all_gather x1, waiting for transfers between devices, on_device(): out_full = lax.all_gather(w_out, 'tm', axis=0, tiled=True)  125 us
    ppermute x2, waiting for transfers between devices, from_behind(): return lax.ppermute(block, axis, route)  48.2 us
    unnamed x6, waiting for transfers between devices  33.6 us
    reduce_scatter x1, waiting for transfers between devices, on_device(): lax.psum_scatter(jnp.concatenate(pieces, axis=0), ('seq', 'mp'), scatter_...  32.9 us
    all_gather x1, waiting for transfers between devices, on_device(): whole = lax.all_gather(hidden, 'seq', axis=1, tiled=True)  25.9 us
  transfers between devices with their start and end apart: 7, of which 7 were waited for; matrix products, arithmetic and copies ran while one was open for 3% of the time, Pallas kernels for 0%

commit v1 on v0

--- a/solution.py
+++ b/solution.py
@@ -8,6 +8,18 @@
 STEPS = 100
 sample_shift = 5.0
 norm_eps = 1e-06
+
+
+def summed_around(x, axis, dim, term):
+    size, position = (lax.axis_size(axis), lax.axis_index(axis))
+    behind = [(i, (i - 1) % size) for i in range(size)]
+    rows = x.shape[dim]
+    held = x
+    so_far = term(held, position * rows)
+    for hop in range(1, size):
+        held = lax.ppermute(held, axis, behind)
+        so_far = so_far + term(held, (position + hop) % size * rows)
+    return so_far
 
 
 def from_behind(block, axis, distance):
@@ -90,11 +102,16 @@
     flat = whole.reshape(frames * seq_len, width)
     head_cols = w_qkv.shape[2]
     heads_dev = head_cols // HEAD_DIM
-    proj = jnp.einsum(
-        "rd,cdh->crh",
-        flat,
-        lax.all_gather(w_qkv, "tm", axis=1, tiled=True),
-        preferred_element_type=jnp.float32,
+    proj = summed_around(
+        w_qkv,
+        "tm",
+        1,
+        lambda shard, at: jnp.einsum(
+            "rd,cdh->crh",
+            lax.dynamic_slice_in_dim(flat, at, shard.shape[1], axis=1),
+            shard,
+            preferred_element_type=jnp.float32,
+        ),
     )
     query = head_norm(proj[0], qk_gain[0], frames, seq_len, heads_dev)
     keys = head_norm(proj[1], qk_gain[1], frames, seq_len, heads_dev)

time: 722 us -> 664 us (0.920)
  waiting for transfers between devices: 664 us -> 561 us
  starting transfers between devices: 2.75 us -> 42.8 us
    all_gather x1 -> x0, waiting for transfers between devices: 398 us -> none  [on_device(): lax.all_gather(w_qkv, 'tm', axis=1, tiled=True)]
    ppermute x0 -> x3, waiting for transfers between devices: none -> 330 us  [summed_around(): held = lax.ppermute(held, axis, behind)]
    all_gather x1, waiting for transfers between devices: 125 us -> 0.02 us  [on_device(): out_full = lax.all_gather(w_out, 'tm', axis=0, tiled=True)]
    unnamed x6 -> x5, waiting for transfers between devices: 33.6 us -> 150 us
    ppermute x0 -> x3, starting transfers between devices: none -> 40.1 us  [summed_around(): held = lax.ppermute(held, axis, behind)]
    all_gather x1, waiting for transfers between devices: 25.9 us -> 0.02 us  [on_device(): whole = lax.all_gather(hidden, 'seq', axis=1, tiled=True)]
    dot_general x1 -> x4, matrix products: 9.97 us -> 14.9 us  [on_device(): jnp.einsum('rd,cdh->crh', lax.dynamic_slice_in_dim(flat, at, shard.shape[...]
  transfers between devices with their start and end apart: 7 -> 9, of which waited for: 7 -> 6; matrix products, arithmetic and copies ran while one was open for 3% -> 4% of each run, Pallas kernels for 0% -> 0%
where the time goes in v1:
time: 664 us
  waiting for transfers between devices  561 us (84%)
  starting transfers between devices  42.8 us (6%)
  matrix products  26.7 us (4%)
  between operations  14.2 us (2%)
  other arithmetic  12.2 us (2%)
    ppermute x3, waiting for transfers between devices, summed_around(): held = lax.ppermute(held, axis, behind)  330 us
    unnamed x5, waiting for transfers between devices  150 us
    ppermute x2, waiting for transfers between devices, from_behind(): return lax.ppermute(block, axis, route)  48.2 us
    ppermute x3, starting transfers between devices, summed_around(): held = lax.ppermute(held, axis, behind)  40.1 us
    reduce_scatter x1, waiting for transfers between devices, on_device(): lax.psum_scatter(jnp.concatenate(pieces, axis=0), ('seq', 'mp'), scatter_...  33.9 us
    dot_general x4, matrix products, on_device(): jnp.einsum('rd,cdh->crh', lax.dynamic_slice_in_dim(flat, at, shard.shape[...  14.9 us
  transfers between devices with their start and end apart: 9, of which 6 were waited for; matrix products, arithmetic and copies ran while one was open for 4% of the time, Pallas kernels for 0%

profile of v1, /device:TPU:25, one launch (start us, length us, event | category | flops | bytes accessed | tf_op | source)
XLA Modules:
  0.0 663.7 jit_solution(14460496490991614508)
XLA Ops:
  10.7 148.8 %all-reduce.3.cloned.1.call-done = f32[4,15360]{1,0:T(4,128)} async-done(((f32[4,15360]{1,0:T(4,128)}), f32[4,15360]{1,0:T(4,128)}) %all-reduce.3.cloned.1.call-update) | async-done | bytes 245776
  159.5 1.6 dynamic-slice_add_fusion
  161.1 1.2 collective-permute-start.1
  164.2 210.2 %collective-permute-done.1 = bf16[3,1280,768]{2,1,0:T(8,128)(2,1)} collective-permute-done((bf16[3,1280,768]{2,1,0:T(8,128)(2,1)}, bf16[3,1280,768]{2,1,0:T(8,128)(2,1)}, u32[]{:S(2)}, u32[]{:S(2)}) %collective-permute-start.1) | collective-permute-done | bytes 5898272 | tf_op jit(solution)/shard_map/ppermute | solution.py:20
  374.4 38.7 %collective-permute-start.2 = (bf16[3,1280,768]{2,1,0:T(8,128)(2,1)}, bf16[3,1280,768]{2,1,0:T(8,128)(2,1)}, u32[]{:S(2)}, u32[]{:S(2)}) collective-permute-start(bf16[3,1280,768]{2,1,0:T(8,128)(2,1)} %collective-permute-done.1), channel_id=1, source_target_pairs={{0,12},{4,0},{8,4},{12,8},{1,13},{5,1},{9,5},{13,9},{2,14},{6,2},{... | collective-permute-start | bytes 17694728 | tf_op jit(solution)/shard_map/ppermute | solution.py:20
  413.2 3.8 fusion.20
  417.0 3.7 convolution_add_fusion.2
  420.7 3.7 convolution_add_fusion.1
  424.4 119.4 %collective-permute-done.2 = bf16[3,1280,768]{2,1,0:T(8,128)(2,1)} collective-permute-done((bf16[3,1280,768]{2,1,0:T(8,128)(2,1)}, bf16[3,1280,768]{2,1,0:T(8,128)(2,1)}, u32[]{:S(2)}, u32[]{:S(2)}) %collective-permute-start.2) | collective-permute-done | bytes 5898272 | tf_op jit(solution)/shard_map/ppermute | solution.py:20
  543.9 3.7 fusion.10
  552.8 3.6 fusion.2
  556.4 3.6 fusion.4
  559.9 1.3 fusion.6
  561.2 1.5 fusion
  562.7 1.7 pad_maximum_fusion
  565.7 1.4 dynamic-slice_reduce_fusion
  567.2 33.9 %reduce-scatter.2.cloned.1.call-done = f32[64,2560]{1,0:T(8,128)} async-done(((f32[256,2560]{1,0:T(8,128)}), f32[64,2560]{1,0:T(8,128)}) %reduce-scatter.2.cloned.1.call-update) | async-done | bytes 655376 | tf_op jit(solution)/shard_map/reduce_scatter | solution.py:135
  601.1 1.8 multiply_multiply_fusion
  602.9 1.3 collective-permute-start.3
  604.2 16.1 %collective-permute-done.3 = f32[64,2560]{1,0:T(8,128)S(1)} collective-permute-done((f32[64,2560]{1,0:T(8,128)S(1)}, f32[64,2560]{1,0:T(8,128)S(1)}, u32[]{:S(2)}, u32[]{:S(2)}) %collective-permute-start.3) | collective-permute-done | bytes 655392 | tf_op jit(solution)/shard_map/ppermute | solution.py:28
  620.3 1.8 fusion.50
  622.1 1.3 collective-permute-start.4
  623.4 32.2 %collective-permute-done.4 = f32[64,2560]{1,0:T(8,128)S(1)} collective-permute-done((f32[64,2560]{1,0:T(8,128)S(1)}, f32[64,2560]{1,0:T(8,128)S(1)}, u32[]{:S(2)}, u32[]{:S(2)}) %collective-permute-start.4) | collective-permute-done | bytes 655392 | tf_op jit(solution)/shard_map/ppermute | solution.py:28
  655.6 1.6 fusion.16
  (53 shorter events, 11.7 us)
Async XLA Ops:
  6.5 1.8 copy-start
  6.5 3.6 copy-start.7
  6.5 3.0 copy-start.2
  6.5 152.9 %all-reduce.3.cloned.1.call-start = ((), (), s32[]{:S(2)}) async-start(), calls=%async_computation.4 | async-start | bytes 491520
  6.5 154.5 %collective-permute-start = (bf16[3,1280,768]{2,1,0:T(8,128)(2,1)}, bf16[3,1280,768]{2,1,0:T(8,128)(2,1)}, u32[]{:S(2)}, u32[]{:S(2)}) collective-permute-start(bf16[3,1280,768]{2,1,0:T(8,128)(2,1)} %param.8), channel_id=1, source_target_pairs={{0,12},{4,0},{8,4},{12,8},{1,13},{5,1},{9,5},{13,9},{2,14},{6,2},{... | collective-permute-start | bytes 17694728 | tf_op jit(solution)/shard_map/ppermute | solution.py:20
  9.5 403.7 %all-gather.3.cloned.1.call-start = ((), (), s32[]{:S(2)}) async-start(), calls=%async_computation.1 | async-start | bytes 1966080 | tf_op jit(solution)/shard_map/all_gather | solution.py:100
  161.1 213.3 %collective-permute-start.1 = (bf16[3,1280,768]{2,1,0:T(8,128)(2,1)}, bf16[3,1280,768]{2,1,0:T(8,128)(2,1)}, u32[]{:S(2)}, u32[]{:S(2)}) collective-permute-start(bf16[3,1280,768]{2,1,0:T(8,128)(2,1)} %collective-permute-done), channel_id=1, source_target_pairs={{0,12},{4,0},{8,4},{12,8},{1,13},{5,1},{9,5},{13,9},{2,14},{6,2},{... | collective-permute-start | bytes 17694728 | tf_op jit(solution)/shard_map/ppermute | solution.py:20
  162.3 250.8 %copy-start.5 = (f32[2,768]{1,0:T(2,128)S(1)}, f32[2,768]{1,0:T(2,128)}, u32[]{:S(2)}) copy-start(f32[2,768]{1,0:T(2,128)} %param.9) | copy-start | bytes 18436
  163.5 389.3 %all-gather.5.cloned.1.call-start = ((), (), s32[]{:S(2)}) async-start(), calls=%async_computation.2 | async-start | bytes 9830400 | tf_op jit(solution)/shard_map/all_gather | solution.py:120
  164.2 436.9 %reduce-scatter.2.cloned.1.call-start = ((), (), s32[]{:S(2)}) async-start(), calls=%async_computation.3 | async-start | bytes 3276800 | tf_op jit(solution)/shard_map/reduce_scatter | solution.py:135
  374.4 169.5 %collective-permute-start.2 = (bf16[3,1280,768]{2,1,0:T(8,128)(2,1)}, bf16[3,1280,768]{2,1,0:T(8,128)(2,1)}, u32[]{:S(2)}, u32[]{:S(2)}) collective-permute-start(bf16[3,1280,768]{2,1,0:T(8,128)(2,1)} %collective-permute-done.1), channel_id=1, source_target_pairs={{0,12},{4,0},{8,4},{12,8},{1,13},{5,1},{9,5},{13,9},{2,14},{6,2},{... | collective-permute-start | bytes 17694728 | tf_op jit(solution)/shard_map/ppermute | solution.py:20
  413.2 3.8 copy-start.4
  552.8 7.2 %copy-start.1 = (bf16[5120,768]{1,0:T(8,128)(2,1)S(1)}, bf16[5120,768]{1,0:T(8,128)(2,1)}, u32[]{:S(2)}) copy-start(bf16[5120,768]{1,0:T(8,128)(2,1)} %all-gather.5.cloned.1.call-done) | copy-start | bytes 23592964
  564.4 0.7 copy-start.6
  601.1 54.5 %copy-start.3 = (f32[64,2560]{1,0:T(8,128)S(1)}, f32[64,2560]{1,0:T(8,128)}, u32[]{:S(2)}) copy-start(f32[64,2560]{1,0:T(8,128)} %reduce-scatter.2.cloned.1.call-done) | copy-start | bytes 1966084
  602.9 17.4 %collective-permute-start.3 = (f32[64,2560]{1,0:T(8,128)S(1)}, f32[64,2560]{1,0:T(8,128)S(1)}, u32[]{:S(2)}, u32[]{:S(2)}) collective-permute-start(f32[64,2560]{1,0:T(8,128)S(1)} %multiply_multiply_fusion), channel_id=1, source_target_pairs={{0,4},{4,8},{8,12},{1,5},{5,9},{9,13},{2,6},{6,10},{10,14},{3,7},{... | collective-permute-start | bytes 1966088 | tf_op jit(solution)/shard_map/ppermute | solution.py:28
  622.1 33.5 %collective-permute-start.4 = (f32[64,2560]{1,0:T(8,128)S(1)}, f32[64,2560]{1,0:T(8,128)S(1)}, u32[]{:S(2)}, u32[]{:S(2)}) collective-permute-start(f32[64,2560]{1,0:T(8,128)S(1)} %fusion.50), channel_id=1, source_target_pairs={{0,8},{4,12},{1,9},{5,13},{2,10},{6,14},{3,11},{7,15},{16,24},{20,... | collective-permute-start | bytes 1966088 | tf_op jit(solution)/shard_map/ppermute | solution.py:28
Sparse Core Ops, SparseCore 0:
  9.7 149.7 all-reduce.2
  163.6 27.2 all-gather.2
  192.5 227.4 all-gather.4
  564.6 36.4 reduce-scatter.1
